TPU v7x, 256 devices: a whole 4x4x8 slice. The times are simulated.
256 devices in a mesh: stream: 4 (over x), seq: 64 (over z, y, core).
Axes of the slice: x: 4, y: 4, z: 8, core: 2. Of those that a mesh axis runs over, the one named last changes fastest.
Arguments:
- inputs: bfloat16 [4, 8192, 2048], P('stream', 'seq'), may hold values from -16 to 16
- cotangent: bfloat16 [4, 8192, 2048], P('stream', 'seq'), may hold values from -6 to 6
- lengths: int32 [4, 4], P('stream'), may hold values from 1 to 6144, 8192 in all within a row
- angles: float32 [2, 2048], replicated, may hold values from -3.140625 to 3.140625
- mix: float32 [14, 2048], replicated, may hold values from -1.5 to 1.5
- weight: bfloat16 [2048, 2048], replicated, may hold values from -0.125 to 0.125
Outputs:
- output: bfloat16 [4, 8192, 2048], P('stream', 'seq')
- input_grad: bfloat16 [4, 8192, 2048], P('stream', 'seq')
- weight_grad: float32 [2048, 2048], P('seq')
- angle_grad: float32 [2, 2048], replicated
- mix_grad: float32 [14, 2048], replicated
Inputs may be any that keep to these rules, and one draw needn't show every extreme that they name: Each row holds the lengths of the 4 documents of one stream in time order; they sum to 8192, and the longest is exactly 6144.
All inputs are finite; a program needn't handle non-finite values.
Results may differ from a plain program's by a relative error of at most 0.012.
Values may be sent and summed in bfloat16 or wider, within the bound.
No kernel may reach another device: no remote copies, remote signals or barrier semaphores. Data moves between devices by JAX's collectives and lax.ppermute only.
A program may use at most 128 MiB of HBM per device.

v0:
```python
import jax
import jax.numpy as jnp
from jax import lax
from jax.sharding import PartitionSpec as P


def from_behind(block, axis, distance):
    devices = range(lax.axis_size(axis))
    route = [(i - distance, i) for i in devices if i - distance in devices]
    return lax.ppermute(block, axis, route)


def segment_start(lengths_row, times):
    ends = jnp.cumsum(lengths_row, dtype=jnp.int32)
    hits = jnp.where(ends[None, :] <= times[:, None], lengths_row[None, :], 0)
    return jnp.sum(hits, axis=1, dtype=jnp.int32)


def tap_mask(times, start, dist):
    return (times - dist >= start).astype(jnp.float32)


def body(inputs, cotangent, lengths, angles, mix, weight):
    local_in = inputs[0]
    local_cot = cotangent[0]
    rows, width = local_in.shape
    seq_count = lax.axis_size("seq")
    stream_count = lax.axis_size("stream")
    far_count = seq_count.bit_length() - 1
    near_count = rows.bit_length() - 1
    levels = near_count + far_count
    total = rows * seq_count
    factor = float(stream_count * total) ** (-0.5)
    member = lax.axis_index("seq")
    cos_a = jnp.cos(angles[0])
    sin_a = jnp.sin(angles[0])
    cos_d = jnp.cos(angles[1])
    sin_d = jnp.sin(angles[1])
    times = member * rows + jnp.arange(rows, dtype=jnp.int32)
    start = segment_start(lengths[0], times)
    masks = [tap_mask(times, start, 2**level)[:, None] for level in range(levels)]
    current = local_in
    stored = [current]
    taps = []
    mixed = jnp.zeros((rows, width), jnp.float32)
    for level in range(near_count):
        dist = 2**level
        before = from_behind(current[rows - dist :], "seq", 1)
        shifted = (
            jnp.concatenate([before, current[: rows - dist]], axis=0).astype(jnp.float32)
            * masks[level]
        )
        plain = current.astype(jnp.float32)
        mixed = mixed + mix[level] * (cos_d * plain + sin_d * shifted)
        current = lax.optimization_barrier((cos_a * plain + sin_a * shifted).astype(jnp.bfloat16))
        taps.append(shifted.astype(jnp.bfloat16))
        stored.append(current)
    for level in range(near_count, levels):
        dist = 2**level
        arrived = from_behind(current, "seq", dist // rows)
        shifted = arrived.astype(jnp.float32) * masks[level]
        plain = current.astype(jnp.float32)
        mixed = mixed + mix[level] * (cos_d * plain + sin_d * shifted)
        current = lax.optimization_barrier((cos_a * plain + sin_a * shifted).astype(jnp.bfloat16))
        taps.append(shifted.astype(jnp.bfloat16))
        stored.append(current)
    mixed = mixed + mix[levels] * current.astype(jnp.float32)
    act = jax.nn.gelu(mixed).astype(jnp.bfloat16)
    output = jnp.dot(act, weight, preferred_element_type=jnp.float32).astype(jnp.bfloat16)
    act_grad = lax.optimization_barrier(
        lax.dot_general(
            local_cot, weight, (((1,), (1,)), ((), ())), preferred_element_type=jnp.float32
        ).astype(jnp.bfloat16)
    )
    unused, pull = jax.vjp(jax.nn.gelu, mixed)
    mixed_grad = lax.optimization_barrier(
        pull(act_grad.astype(jnp.float32))[0].astype(jnp.bfloat16)
    )
    grad_full = mixed_grad.astype(jnp.float32)
    upper = mix[levels] * grad_full
    mix_rows = [None] * (levels + 1)
    mix_rows[levels] = jnp.sum(grad_full * stored[levels].astype(jnp.float32), axis=0)
    theta = jnp.zeros((width,), jnp.float32)
    phi = jnp.zeros((width,), jnp.float32)
    carried = stored[0]
    for level in reversed(range(levels)):
        dist = 2**level
        plain = stored[level].astype(jnp.float32)
        shifted = taps[level].astype(jnp.float32)
        along = mix[level] * grad_full
        mix_rows[level] = jnp.sum(grad_full * (cos_d * plain + sin_d * shifted), axis=0)
        theta = theta + jnp.sum(upper * (cos_a * shifted - sin_a * plain), axis=0)
        phi = phi + jnp.sum(along * (cos_d * shifted - sin_d * plain), axis=0)
        sent = lax.optimization_barrier(
            (masks[level] * (sin_a * upper + sin_d * along)).astype(jnp.bfloat16)
        )
        if dist < rows:
            after = from_behind(sent[:dist], "seq", -1)
            back = jnp.concatenate([sent[dist:], after], axis=0)
        else:
            back = from_behind(sent, "seq", -(dist // rows))
        carried = lax.optimization_barrier(
            (cos_a * upper + cos_d * along + back.astype(jnp.float32)).astype(jnp.bfloat16)
        )
        upper = carried.astype(jnp.float32)
    angle_all, mix_all = lax.psum((jnp.stack([theta, phi]), jnp.stack(mix_rows)), ("stream", "seq"))
    weight_rows = lax.psum_scatter(
        lax.dot_general(
            act, local_cot, (((0,), (0,)), ((), ())), preferred_element_type=jnp.float32
        ),
        "seq",
        scatter_dimension=0,
        tiled=True,
    )
    weight_rows = lax.psum(weight_rows, "stream")
    return (output[None], carried[None], weight_rows * factor, angle_all * factor, mix_all * factor)


def solution(mesh):
    in_specs = (
        P("stream", "seq", None),
        P("stream", "seq", None),
        P("stream", None),
        P(),
        P(),
        P(),
    )
    out_specs = (P("stream", "seq", None), P("stream", "seq", None), P("seq", None), P(), P())
    return jax.shard_map(body, mesh=mesh, in_specs=in_specs, out_specs=out_specs, check_vma=False)
```

profile of v0, /device:TPU:8, one launch (start us, length us, event | category | flops | bytes accessed | tf_op | source)
XLA Modules:
  0.0 812.0 jit_solution(9908100230172136991)
XLA Ops:
  8.9 1.9 collective-permute-start
  11.9 1.9 slice_cosine_fusion.1
  17.4 3.6 collective-permute-start.1
  23.6 1.9 collective-permute-start.2
  25.5 3.1 collective-permute-done.2
  29.7 1.9 collective-permute-start.3
  31.6 3.3 collective-permute-done.3
  35.9 2.1 collective-permute-start.4
  38.0 3.6 collective-permute-done.4
  42.6 1.9 collective-permute-start.5
  44.5 4.3 collective-permute-done.5
  49.8 1.9 collective-permute-start.6
  51.7 5.8 collective-permute-done.6
  58.5 2.1 collective-permute-start.7
  60.6 8.6 %collective-permute-done.7 = bf16[128,2048]{1,0:T(8,128)(2,1)S(1)} collective-permute-done((bf16[128,2048]{1,0:T(8,128)(2,1)S(1)}, bf16[128,2048]{1,0:T(8,128)(2,1)S(1)}, u32[]{:S(2)}, u32[]{:S(2)}) %collective-permute-start.7) | collective-permute-done | bytes 524320 | tf_op jit(solution)/shard_map/ppermute | solution.py:10
  70.1 3.5 collective-permute-start.8
  73.6 11.4 %collective-permute-done.8 = bf16[128,2048]{1,0:T(8,128)(2,1)S(1)} collective-permute-done((bf16[128,2048]{1,0:T(8,128)(2,1)S(1)}, bf16[128,2048]{1,0:T(8,128)(2,1)S(1)}, u32[]{:S(2)}, u32[]{:S(2)}) %collective-permute-start.8) | collective-permute-done | bytes 524320 | tf_op jit(solution)/shard_map/ppermute | solution.py:10
  86.0 15.0 %collective-permute-start.9 = (bf16[128,2048]{1,0:T(8,128)(2,1)S(1)}, bf16[128,2048]{1,0:T(8,128)(2,1)S(1)}, u32[]{:S(2)}, u32[]{:S(2)}) collective-permute-start(bf16[128,2048]{1,0:T(8,128)(2,1)S(1)} %fusion.250), channel_id=1, source_target_pairs={{0,4},{1,5},{2,6},{3,7},{4,8},{5,9},{6,10},{7,11},{8,12},{9,13},{1... | collective-permute-start | bytes 1572872 | tf_op jit(solution)/shard_map/ppermute | solution.py:10
  101.0 7.5 collective-permute-done.9
  109.4 4.3 collective-permute-start.10
  113.8 6.6 collective-permute-done.10
  121.4 14.6 %collective-permute-start.11 = (bf16[128,2048]{1,0:T(8,128)(2,1)S(1)}, bf16[128,2048]{1,0:T(8,128)(2,1)S(1)}, u32[]{:S(2)}, u32[]{:S(2)}) collective-permute-start(bf16[128,2048]{1,0:T(8,128)(2,1)S(1)} %fusion.254), channel_id=1, source_target_pairs={{0,16},{1,17},{2,18},{3,19},{4,20},{5,21},{6,22},{7,23},{8,24},{9,... | collective-permute-start | bytes 1572872 | tf_op jit(solution)/shard_map/ppermute | solution.py:10
  136.0 8.1 collective-permute-done.11
  145.0 31.3 %collective-permute-start.12 = (bf16[128,2048]{1,0:T(8,128)(2,1)S(1)}, bf16[128,2048]{1,0:T(8,128)(2,1)S(1)}, u32[]{:S(2)}, u32[]{:S(2)}) collective-permute-start(bf16[128,2048]{1,0:T(8,128)(2,1)S(1)} %fusion.256), channel_id=1, source_target_pairs={{0,32},{1,33},{2,34},{3,35},{4,36},{5,37},{6,38},{7,39},{8,40},{9,... | collective-permute-start | bytes 1572872 | tf_op jit(solution)/shard_map/ppermute | solution.py:10
  176.4 2.9 convolution_convert_fusion
  179.5 7.8 collective-permute-done.12
  188.4 7.4 fusion.97
  197.1 8.1 %fusion.288 = f32[2048,2048]{1,0:T(8,128)} fusion(bf16[1,128,2048]{2,1,0:T(8,128)(2,1)S(1)} %copy-done, f32[128,2048]{1,0:T(8,128)S(1)} %get-tuple-element.55), kind=kOutput, calls=%fused_computation.471 | convolution fusion | flops 1076101120 | bytes 18350080 | tf_op jit(solution)/shard_map/dot_general | solution.py:108
  208.0 19.3 %collective-permute-done.13 = bf16[128,2048]{1,0:T(8,128)(2,1)S(1)} collective-permute-done((bf16[128,2048]{1,0:T(8,128)(2,1)S(1)}, bf16[128,2048]{1,0:T(8,128)(2,1)S(1)}, u32[]{:S(2)}, u32[]{:S(2)}) %collective-permute-start.13) | collective-permute-done | bytes 524320 | tf_op jit(solution)/shard_map/ppermute | solution.py:10
  230.6 26.2 %collective-permute-done.14 = bf16[128,2048]{1,0:T(8,128)(2,1)S(1)} collective-permute-done((bf16[128,2048]{1,0:T(8,128)(2,1)S(1)}, bf16[128,2048]{1,0:T(8,128)(2,1)S(1)}, u32[]{:S(2)}, u32[]{:S(2)}) %collective-permute-start.14) | collective-permute-done | bytes 524320 | tf_op jit(solution)/shard_map/ppermute | solution.py:10
  260.5 13.7 %collective-permute-done.15 = bf16[128,2048]{1,0:T(8,128)(2,1)S(1)} collective-permute-done((bf16[128,2048]{1,0:T(8,128)(2,1)S(1)}, bf16[128,2048]{1,0:T(8,128)(2,1)S(1)}, u32[]{:S(2)}, u32[]{:S(2)}) %collective-permute-start.15) | collective-permute-done | bytes 524320 | tf_op jit(solution)/shard_map/ppermute | solution.py:10
  275.4 3.1 fusion.270
  279.7 19.8 %collective-permute-done.16 = bf16[128,2048]{1,0:T(8,128)(2,1)S(1)} collective-permute-done((bf16[128,2048]{1,0:T(8,128)(2,1)S(1)}, bf16[128,2048]{1,0:T(8,128)(2,1)S(1)}, u32[]{:S(2)}, u32[]{:S(2)}) %collective-permute-start.16) | collective-permute-done | bytes 524320 | tf_op jit(solution)/shard_map/ppermute | solution.py:10
  299.9 3.1 fusion.269
  303.0 10.8 %collective-permute-start.17 = (bf16[128,2048]{1,0:T(8,128)(2,1)S(1)}, bf16[128,2048]{1,0:T(8,128)(2,1)S(1)}, u32[]{:S(2)}, u32[]{:S(2)}) collective-permute-start(bf16[128,2048]{1,0:T(8,128)(2,1)S(1)} %get-tuple-element.57), channel_id=1, source_target_pairs={{2,0},{3,1},{4,2},{5,3},{6,4},{7,5},{8,6},{9,7},{10,8},{11,9},{12,... | collective-permute-start | bytes 1572872 | tf_op jit(solution)/shard_map/ppermute | solution.py:10
  313.9 22.7 %collective-permute-done.17 = bf16[128,2048]{1,0:T(8,128)(2,1)S(1)} collective-permute-done((bf16[128,2048]{1,0:T(8,128)(2,1)S(1)}, bf16[128,2048]{1,0:T(8,128)(2,1)S(1)}, u32[]{:S(2)}, u32[]{:S(2)}) %collective-permute-start.17) | collective-permute-done | bytes 524320 | tf_op jit(solution)/shard_map/ppermute | solution.py:10
  337.0 3.0 fusion.268
  340.0 1.9 collective-permute-start.18
  341.9 6.7 collective-permute-done.18
  348.9 2.2 fusion.267
  351.2 4.2 collective-permute-start.19
  355.4 3.9 collective-permute-done.19
  359.6 2.2 fusion.266
  361.8 4.2 collective-permute-start.20
  366.1 5.5 collective-permute-done.20
  371.9 1.6 fusion.265
  373.5 3.4 collective-permute-start.21
  376.9 5.1 collective-permute-done.21
  382.4 1.6 fusion.264
  384.0 1.9 collective-permute-start.22
  386.0 3.6 collective-permute-done.22
  389.9 1.9 fusion.263
  391.8 1.9 collective-permute-start.23
  393.8 3.1 collective-permute-done.23
  397.3 1.8 fusion.262
  399.2 2.1 collective-permute-start.24
  401.3 2.3 fusion
  404.8 1.8 fusion.261
  406.6 2.2 collective-permute-start.25
  408.9 101.6 %psum.22 = f32[2,2048]{1,0:T(2,128)S(1)} all-reduce(f32[2,2048]{1,0:T(2,128)S(1)} %pad_maximum_fusion.7), channel_id=1, replica_groups=mesh['stream'=4,'seq'=64] {'stream','seq'}, use_global_device_ids=true, to_apply=%region_30.31 | all-reduce | flops 4096 | bytes 32768 | tf_op jit(solution)/shard_map/psum | solution.py:106
  514.0 243.3 %all-reduce.5.cloned.1.call-done = f32[14,2048]{1,0:T(8,128)} async-done(((f32[14,2048]{1,0:T(8,128)}), f32[14,2048]{1,0:T(8,128)}) %all-reduce.5.cloned.1.call-update) | async-done | bytes 114704 | tf_op jit(solution)/shard_map/psum | solution.py:106
  757.2 1.6 broadcast_multiply_fusion.1
  758.8 43.9 %all-reduce.3.cloned.1.call-done = f32[32,2048]{1,0:T(8,128)} async-done(((f32[32,2048]{1,0:T(8,128)}), f32[32,2048]{1,0:T(8,128)}) %all-reduce.3.cloned.1.call-update) | async-done | bytes 262160 | tf_op jit(solution)/shard_map/psum | solution.py:115
  802.7 1.7 broadcast_multiply_fusion
  (286 shorter events, 39.0 us)
Async XLA Ops:
  8.0 168.4 %copy-start = (bf16[1,128,2048]{2,1,0:T(8,128)(2,1)S(1)}, bf16[1,128,2048]{2,1,0:T(8,128)(2,1)}, u32[]{:S(2)}) copy-start(bf16[1,128,2048]{2,1,0:T(8,128)(2,1)} %param.7) | copy-start | bytes 1572868
  8.0 505.9 %reduce-scatter.2.cloned.1.call-start = ((), (), s32[]{:S(2)}) async-start(), calls=%async_computation.1 | async-start | bytes 17039360 | tf_op jit(solution)/shard_map/reduce_scatter | solution.py:107
  8.9 7.1 collective-permute-start
  17.4 5.1 collective-permute-start.1
  23.6 5.1 collective-permute-start.2
  28.6 159.6 %copy-start.65 = (bf16[4,2048]{1,0:T(4,128)(2,1)}, bf16[4,2048]{1,0:T(4,128)(2,1)S(1)}, u32[]{:S(2)}) copy-start(bf16[4,2048]{1,0:T(4,128)(2,1)S(1)} %collective-permute-done.2) | copy-start | bytes 49156
  29.7 5.2 collective-permute-start.3
  31.6 156.6 %copy-start.22 = (bf16[120,2048]{1,0:T(8,128)(2,1)}, bf16[120,2048]{1,0:T(8,128)(2,1)S(1)}, u32[]{:S(2)}) copy-start(bf16[120,2048]{1,0:T(8,128)(2,1)S(1)} %slice.205) | copy-start | bytes 1474564
  34.9 153.4 %copy-start.55 = (bf16[8,2048]{1,0:T(8,128)(2,1)}, bf16[8,2048]{1,0:T(8,128)(2,1)S(1)}, u32[]{:S(2)}) copy-start(bf16[8,2048]{1,0:T(8,128)(2,1)S(1)} %collective-permute-done.3) | copy-start | bytes 98308
  34.9 141.5 %slice-start = ((s8[8388608]{0:T(1024)(128)(4,1)}), s8[4194304]{0:T(1024)(128)(4,1)S(1)}, s32[]{:S(2)}) async-start(s8[8388608]{0:T(1024)(128)(4,1)} %bitcast.103), calls=%async_computation.4 | async-start | bytes 8388608
  35.9 5.7 collective-permute-start.4
  38.0 150.2 %copy-start.24 = (bf16[112,2048]{1,0:T(8,128)(2,1)}, bf16[112,2048]{1,0:T(8,128)(2,1)S(1)}, u32[]{:S(2)}) copy-start(bf16[112,2048]{1,0:T(8,128)(2,1)S(1)} %slice.207) | copy-start | bytes 1376260
  41.7 146.6 %copy-start.53 = (bf16[16,2048]{1,0:T(8,128)(2,1)}, bf16[16,2048]{1,0:T(8,128)(2,1)S(1)}, u32[]{:S(2)}) copy-start(bf16[16,2048]{1,0:T(8,128)(2,1)S(1)} %collective-permute-done.4) | copy-start | bytes 196612
  42.5 145.8 %copy-start.1 = (bf16[128,2048]{1,0:T(8,128)(2,1)}, bf16[128,2048]{1,0:T(8,128)(2,1)S(1)}, u32[]{:S(2)}) copy-start(bf16[128,2048]{1,0:T(8,128)(2,1)S(1)} %fusion.242) | copy-start | bytes 1572868
  42.6 6.3 collective-permute-start.5
  48.8 139.5 %copy-start.51 = (bf16[32,2048]{1,0:T(8,128)(2,1)}, bf16[32,2048]{1,0:T(8,128)(2,1)S(1)}, u32[]{:S(2)}) copy-start(bf16[32,2048]{1,0:T(8,128)(2,1)S(1)} %collective-permute-done.5) | copy-start | bytes 393220
  49.7 138.6 %copy-start.3 = (bf16[128,2048]{1,0:T(8,128)(2,1)}, bf16[128,2048]{1,0:T(8,128)(2,1)S(1)}, u32[]{:S(2)}) copy-start(bf16[128,2048]{1,0:T(8,128)(2,1)S(1)} %fusion.244) | copy-start | bytes 1572868
  49.8 138.6 %copy-start.43 = (bf16[64,2048]{1,0:T(8,128)(2,1)}, bf16[64,2048]{1,0:T(8,128)(2,1)S(1)}, u32[]{:S(2)}) copy-start(bf16[64,2048]{1,0:T(8,128)(2,1)S(1)} %get-tuple-element.69) | copy-start | bytes 786436
  49.8 7.7 collective-permute-start.6
  57.5 130.9 %copy-start.47 = (bf16[64,2048]{1,0:T(8,128)(2,1)}, bf16[64,2048]{1,0:T(8,128)(2,1)S(1)}, u32[]{:S(2)}) copy-start(bf16[64,2048]{1,0:T(8,128)(2,1)S(1)} %collective-permute-done.6) | copy-start | bytes 786436
  57.5 118.9 %slice-start.1 = ((s8[8388608]{0:T(1024)(128)(4,1)}), s8[4194304]{0:T(1024)(128)(4,1)S(1)}, s32[]{:S(2)}) async-start(s8[8388608]{0:T(1024)(128)(4,1)} %bitcast.103), calls=%async_computation.5 | async-start | bytes 8388608
  58.5 129.9 %copy-start.18 = (bf16[128,2048]{1,0:T(8,128)(2,1)}, bf16[128,2048]{1,0:T(8,128)(2,1)S(1)}, u32[]{:S(2)}) copy-start(bf16[128,2048]{1,0:T(8,128)(2,1)S(1)} %fusion.246) | copy-start | bytes 1572868
  58.5 10.6 %collective-permute-start.7 = (bf16[128,2048]{1,0:T(8,128)(2,1)S(1)}, bf16[128,2048]{1,0:T(8,128)(2,1)S(1)}, u32[]{:S(2)}, u32[]{:S(2)}) collective-permute-start(bf16[128,2048]{1,0:T(8,128)(2,1)S(1)} %fusion.246), channel_id=1, source_target_pairs={{0,1},{1,2},{2,3},{3,4},{4,5},{5,6},{6,7},{7,8},{8,9},{9,10},{10,1... | collective-permute-start | bytes 1572872 | tf_op jit(solution)/shard_map/ppermute | solution.py:10
  69.1 119.2 %copy-start.39 = (bf16[128,2048]{1,0:T(8,128)(2,1)}, bf16[128,2048]{1,0:T(8,128)(2,1)S(1)}, u32[]{:S(2)}) copy-start(bf16[128,2048]{1,0:T(8,128)(2,1)S(1)} %collective-permute-done.7) | copy-start | bytes 1572868
  69.1 110.1 %copy-start.87 = (f32[14,2048]{1,0:T(8,128)S(1)}, f32[14,2048]{1,0:T(8,128)}, u32[]{:S(2)}) copy-start(f32[14,2048]{1,0:T(8,128)} %param.10) | copy-start | bytes 344068
  70.1 118.3 %copy-start.7 = (bf16[128,2048]{1,0:T(8,128)(2,1)}, bf16[128,2048]{1,0:T(8,128)(2,1)S(1)}, u32[]{:S(2)}) copy-start(bf16[128,2048]{1,0:T(8,128)(2,1)S(1)} %fusion.248) | copy-start | bytes 1572868
  70.1 14.9 %collective-permute-start.8 = (bf16[128,2048]{1,0:T(8,128)(2,1)S(1)}, bf16[128,2048]{1,0:T(8,128)(2,1)S(1)}, u32[]{:S(2)}, u32[]{:S(2)}) collective-permute-start(bf16[128,2048]{1,0:T(8,128)(2,1)S(1)} %fusion.248), channel_id=1, source_target_pairs={{0,2},{1,3},{2,4},{3,5},{4,6},{5,7},{6,8},{7,9},{8,10},{9,11},{10,... | collective-permute-start | bytes 1572872 | tf_op jit(solution)/shard_map/ppermute | solution.py:10
  85.0 103.4 %copy-start.29 = (bf16[128,2048]{1,0:T(8,128)(2,1)}, bf16[128,2048]{1,0:T(8,128)(2,1)S(1)}, u32[]{:S(2)}) copy-start(bf16[128,2048]{1,0:T(8,128)(2,1)S(1)} %collective-permute-done.8) | copy-start | bytes 1572868
  85.9 109.9 %copy-start.11 = (bf16[128,2048]{1,0:T(8,128)(2,1)}, bf16[128,2048]{1,0:T(8,128)(2,1)S(1)}, u32[]{:S(2)}) copy-start(bf16[128,2048]{1,0:T(8,128)(2,1)S(1)} %fusion.250) | copy-start | bytes 1572868
  85.9 102.4 %copy-start.5 = (bf16[1,128,2048]{2,1,0:T(8,128)(2,1)S(1)}, bf16[1,128,2048]{2,1,0:T(8,128)(2,1)}, u32[]{:S(2)}) copy-start(bf16[1,128,2048]{2,1,0:T(8,128)(2,1)} %param.6) | copy-start | bytes 1572868
  86.0 102.4 %copy-start.16 = (bf16[127,2048]{1,0:T(8,128)(2,1)S(1)}, bf16[127,2048]{1,0:T(8,128)(2,1)}, u32[]{:S(2)}) copy-start(bf16[127,2048]{1,0:T(8,128)(2,1)} %copy-done.15) | copy-start | bytes 1560580
  86.0 102.4 %copy-start.26 = (f32[1,2048]{1,0:T(1,128)S(1)}, f32[1,2048]{1,0:T(1,128)}, u32[]{:S(2)}) copy-start(f32[1,2048]{1,0:T(1,128)} %get-tuple-element.84) | copy-start | bytes 24580
  86.0 102.4 %copy-start.49 = (f32[1,2048]{1,0:T(1,128)S(1)}, f32[1,2048]{1,0:T(1,128)}, u32[]{:S(2)}) copy-start(f32[1,2048]{1,0:T(1,128)} %get-tuple-element.85) | copy-start | bytes 24580
  86.0 102.4 %copy-start.89 = (bf16[1,2048]{1,0:T(2,128)(2,1)S(1)}, bf16[1,2048]{1,0:T(2,128)(2,1)}, u32[]{:S(2)}) copy-start(bf16[1,2048]{1,0:T(2,128)(2,1)} %copy-done.88) | copy-start | bytes 12292
  86.0 22.5 %collective-permute-start.9 = (bf16[128,2048]{1,0:T(8,128)(2,1)S(1)}, bf16[128,2048]{1,0:T(8,128)(2,1)S(1)}, u32[]{:S(2)}, u32[]{:S(2)}) collective-permute-start(bf16[128,2048]{1,0:T(8,128)(2,1)S(1)} %fusion.250), channel_id=1, source_target_pairs={{0,4},{1,5},{2,6},{3,7},{4,8},{5,9},{6,10},{7,11},{8,12},{9,13},{1... | collective-permute-start | bytes 1572872 | tf_op jit(solution)/shard_map/ppermute | solution.py:10
  109.4 11.0 %collective-permute-start.10 = (bf16[128,2048]{1,0:T(8,128)(2,1)S(1)}, bf16[128,2048]{1,0:T(8,128)(2,1)S(1)}, u32[]{:S(2)}, u32[]{:S(2)}) collective-permute-start(bf16[128,2048]{1,0:T(8,128)(2,1)S(1)} %fusion.252), channel_id=1, source_target_pairs={{0,8},{1,9},{2,10},{3,11},{4,12},{5,13},{6,14},{7,15},{8,16},{9,17... | collective-permute-start | bytes 1572872 | tf_op jit(solution)/shard_map/ppermute | solution.py:10
  121.4 22.7 %collective-permute-start.11 = (bf16[128,2048]{1,0:T(8,128)(2,1)S(1)}, bf16[128,2048]{1,0:T(8,128)(2,1)S(1)}, u32[]{:S(2)}, u32[]{:S(2)}) collective-permute-start(bf16[128,2048]{1,0:T(8,128)(2,1)S(1)} %fusion.254), channel_id=1, source_target_pairs={{0,16},{1,17},{2,18},{3,19},{4,20},{5,21},{6,22},{7,23},{8,24},{9,... | collective-permute-start | bytes 1572872 | tf_op jit(solution)/shard_map/ppermute | solution.py:10
  145.0 42.4 %collective-permute-start.12 = (bf16[128,2048]{1,0:T(8,128)(2,1)S(1)}, bf16[128,2048]{1,0:T(8,128)(2,1)S(1)}, u32[]{:S(2)}, u32[]{:S(2)}) collective-permute-start(bf16[128,2048]{1,0:T(8,128)(2,1)S(1)} %fusion.256), channel_id=1, source_target_pairs={{0,32},{1,33},{2,34},{3,35},{4,36},{5,37},{6,38},{7,39},{8,40},{9,... | collective-permute-start | bytes 1572872 | tf_op jit(solution)/shard_map/ppermute | solution.py:10
  205.2 552.0 %all-reduce.5.cloned.1.call-start = ((), (), s32[]{:S(2)}) async-start(), calls=%async_computation.3 | async-start | bytes 262144 | tf_op jit(solution)/shard_map/psum | solution.py:106
  205.4 94.5 %copy-start.8 = (bf16[128,2048]{1,0:T(8,128)(2,1)S(1)}, bf16[128,2048]{1,0:T(8,128)(2,1)}, u32[]{:S(2)}) copy-start(bf16[128,2048]{1,0:T(8,128)(2,1)} %copy-done.7) | copy-start | bytes 1572868
  205.4 94.5 %copy-start.10 = (bf16[128,2048]{1,0:T(8,128)(2,1)S(1)}, bf16[128,2048]{1,0:T(8,128)(2,1)}, u32[]{:S(2)}) copy-start(bf16[128,2048]{1,0:T(8,128)(2,1)} %copy-done.9) | copy-start | bytes 1572868
  206.6 20.8 %collective-permute-start.13 = (bf16[128,2048]{1,0:T(8,128)(2,1)S(1)}, bf16[128,2048]{1,0:T(8,128)(2,1)S(1)}, u32[]{:S(2)}, u32[]{:S(2)}) collective-permute-start(bf16[128,2048]{1,0:T(8,128)(2,1)S(1)} %fusion.189), channel_id=1, source_target_pairs={{32,0},{33,1},{34,2},{35,3},{36,4},{37,5},{38,6},{39,7},{40,8},{41... | collective-permute-start | bytes 1572872 | tf_op jit(solution)/shard_map/ppermute | solution.py:10
  229.3 27.5 %collective-permute-start.14 = (bf16[128,2048]{1,0:T(8,128)(2,1)S(1)}, bf16[128,2048]{1,0:T(8,128)(2,1)S(1)}, u32[]{:S(2)}, u32[]{:S(2)}) collective-permute-start(bf16[128,2048]{1,0:T(8,128)(2,1)S(1)} %fusion.182), channel_id=1, source_target_pairs={{16,0},{17,1},{18,2},{19,3},{20,4},{21,5},{22,6},{23,7},{24,8},{25... | collective-permute-start | bytes 1572872 | tf_op jit(solution)/shard_map/ppermute | solution.py:10
  259.1 15.1 %collective-permute-start.15 = (bf16[128,2048]{1,0:T(8,128)(2,1)S(1)}, bf16[128,2048]{1,0:T(8,128)(2,1)S(1)}, u32[]{:S(2)}, u32[]{:S(2)}) collective-permute-start(bf16[128,2048]{1,0:T(8,128)(2,1)S(1)} %fusion.175), channel_id=1, source_target_pairs={{8,0},{9,1},{10,2},{11,3},{12,4},{13,5},{14,6},{15,7},{16,8},{17,9... | collective-permute-start | bytes 1572872 | tf_op jit(solution)/shard_map/ppermute | solution.py:10
  278.5 21.1 %collective-permute-start.16 = (bf16[128,2048]{1,0:T(8,128)(2,1)S(1)}, bf16[128,2048]{1,0:T(8,128)(2,1)S(1)}, u32[]{:S(2)}, u32[]{:S(2)}) collective-permute-start(bf16[128,2048]{1,0:T(8,128)(2,1)S(1)} %get-tuple-element.56), channel_id=1, source_target_pairs={{4,0},{5,1},{6,2},{7,3},{8,4},{9,5},{10,6},{11,7},{12,8},{13,9},{1... | collective-permute-start | bytes 1572872 | tf_op jit(solution)/shard_map/ppermute | solution.py:10
  303.0 33.5 %collective-permute-start.17 = (bf16[128,2048]{1,0:T(8,128)(2,1)S(1)}, bf16[128,2048]{1,0:T(8,128)(2,1)S(1)}, u32[]{:S(2)}, u32[]{:S(2)}) collective-permute-start(bf16[128,2048]{1,0:T(8,128)(2,1)S(1)} %get-tuple-element.57), channel_id=1, source_target_pairs={{2,0},{3,1},{4,2},{5,3},{6,4},{7,5},{8,6},{9,7},{10,8},{11,9},{12,... | collective-permute-start | bytes 1572872 | tf_op jit(solution)/shard_map/ppermute | solution.py:10
  340.0 8.6 %collective-permute-start.18 = (bf16[128,2048]{1,0:T(8,128)(2,1)S(1)}, bf16[128,2048]{1,0:T(8,128)(2,1)S(1)}, u32[]{:S(2)}, u32[]{:S(2)}) collective-permute-start(bf16[128,2048]{1,0:T(8,128)(2,1)S(1)} %get-tuple-element.58), channel_id=1, source_target_pairs={{1,0},{2,1},{3,2},{4,3},{5,4},{6,5},{7,6},{8,7},{9,8},{10,9},{11,1... | collective-permute-start | bytes 1572872 | tf_op jit(solution)/shard_map/ppermute | solution.py:10
  351.2 8.1 collective-permute-start.19
  361.8 9.7 %collective-permute-start.20 = (bf16[32,2048]{1,0:T(8,128)(2,1)S(1)}, bf16[32,2048]{1,0:T(8,128)(2,1)S(1)}, u32[]{:S(2)}, u32[]{:S(2)}) collective-permute-start(bf16[32,2048]{1,0:T(8,128)(2,1)S(1)} %slice.215), channel_id=1, source_target_pairs={{1,0},{2,1},{3,2},{4,3},{5,4},{6,5},{7,6},{8,7},{9,8},{10,9},{11,1... | collective-permute-start | bytes 393224 | tf_op jit(solution)/shard_map/ppermute | solution.py:10
  373.5 8.6 %collective-permute-start.21 = (bf16[16,2048]{1,0:T(8,128)(2,1)S(1)}, bf16[16,2048]{1,0:T(8,128)(2,1)S(1)}, u32[]{:S(2)}, u32[]{:S(2)}) collective-permute-start(bf16[16,2048]{1,0:T(8,128)(2,1)S(1)} %slice.217), channel_id=1, source_target_pairs={{1,0},{2,1},{3,2},{4,3},{5,4},{6,5},{7,6},{8,7},{9,8},{10,9},{11,1... | collective-permute-start | bytes 196616 | tf_op jit(solution)/shard_map/ppermute | solution.py:10
  384.0 5.5 collective-permute-start.22
  391.8 5.2 collective-permute-start.23
  399.1 112.1 %copy-start.91 = (f32[2048]{0:T(1024)S(1)}, f32[2048]{0:T(1024)}, u32[]{:S(2)}) copy-start(f32[2048]{0:T(1024)} %get-tuple-element.17) | copy-start | bytes 24580
  399.2 112.1 %copy-start.92 = (f32[2048]{0:T(1024)S(1)}, f32[2048]{0:T(1024)}, u32[]{:S(2)}) copy-start(f32[2048]{0:T(1024)} %get-tuple-element.52) | copy-start | bytes 24580
  399.2 112.1 %copy-start.93 = (f32[2048]{0:T(1024)S(1)}, f32[2048]{0:T(1024)}, u32[]{:S(2)}) copy-start(f32[2048]{0:T(1024)} %get-tuple-element.19) | copy-start | bytes 24580
  399.2 112.1 %copy-start.94 = (f32[2048]{0:T(1024)S(1)}, f32[2048]{0:T(1024)}, u32[]{:S(2)}) copy-start(f32[2048]{0:T(1024)} %get-tuple-element.49) | copy-start | bytes 24580
  399.2 112.1 %copy-start.95 = (f32[2048]{0:T(1024)S(1)}, f32[2048]{0:T(1024)}, u32[]{:S(2)}) copy-start(f32[2048]{0:T(1024)} %get-tuple-element.21) | copy-start | bytes 24580
  399.2 112.1 %copy-start.96 = (f32[2048]{0:T(1024)S(1)}, f32[2048]{0:T(1024)}, u32[]{:S(2)}) copy-start(f32[2048]{0:T(1024)} %get-tuple-element.46) | copy-start | bytes 24580
  399.2 112.1 %copy-start.97 = (f32[2048]{0:T(1024)S(1)}, f32[2048]{0:T(1024)}, u32[]{:S(2)}) copy-start(f32[2048]{0:T(1024)} %get-tuple-element.23) | copy-start | bytes 24580
  399.2 112.1 %copy-start.98 = (f32[2048]{0:T(1024)S(1)}, f32[2048]{0:T(1024)}, u32[]{:S(2)}) copy-start(f32[2048]{0:T(1024)} %get-tuple-element.25) | copy-start | bytes 24580
  399.2 113.6 %copy-start.28 = (f32[1,2048]{1,0:T(1,128)S(1)}, f32[1,2048]{1,0:T(1,128)}, u32[]{:S(2)}) copy-start(f32[1,2048]{1,0:T(1,128)} %get-tuple-element.84) | copy-start | bytes 24580
  399.2 5.2 collective-permute-start.24
  406.6 106.2 %collective-permute-start.25 = (bf16[1,2048]{1,0:T(2,128)(2,1)S(1)}, bf16[1,2048]{1,0:T(2,128)(2,1)S(1)}, u32[]{:S(2)}, u32[]{:S(2)}) collective-permute-start(bf16[1,2048]{1,0:T(2,128)(2,1)S(1)} %slice.225), channel_id=1, source_target_pairs={{1,0},{2,1},{3,2},{4,3},{5,4},{6,5},{7,6},{8,7},{9,8},{10,9},{11,1... | collective-permute-start | bytes 12296 | tf_op jit(solution)/shard_map/ppermute | solution.py:10
  512.7 289.9 %all-reduce.3.cloned.1.call-start = ((), (), s32[]{:S(2)}) async-start(), calls=%async_computation.2 | async-start | bytes 524288 | tf_op jit(solution)/shard_map/psum | solution.py:115
  (68 other events, 3083.7 us)
Sparse Core Ops, SparseCore 0:
  205.4 223.6 reduce-scatter.1
Sparse Core Ops, SparseCore 1:
  512.8 244.4 all-reduce.4
  759.4 43.2 all-reduce.2
where the time goes:
time: 819 us; the launch traced here: 812 us
  waiting for transfers between devices  489 us (60%)
  starting transfers between devices  124 us (15%)
  blocking collectives  102 us (12%)
  other arithmetic  58.4 us (7%)
  between operations  17.8 us (2%)
  matrix products  13.3 us (2%)
    psum x1, waiting for transfers between devices, body(): lax.psum((jnp.stack([theta, phi]), jnp.stack(mix_rows)), ('stream', 'seq'))  243 us
    ppermute x26, waiting for transfers between devices, from_behind(): return lax.ppermute(block, axis, route)  202 us
    ppermute x26, starting transfers between devices, from_behind(): return lax.ppermute(block, axis, route)  124 us
    psum x1, blocking collectives, body(): lax.psum((jnp.stack([theta, phi]), jnp.stack(mix_rows)), ('stream', 'seq'))  102 us
    psum x1, waiting for transfers between devices, body(): weight_rows = lax.psum(weight_rows, 'stream')  43.9 us
    reduce_sum x10, other arithmetic, body(): jnp.sum(grad_full * (cos_d * plain + sin_d * shifted), axis=0)  22.1 us
  transfers between devices with their start and end apart: 29, of which 26 were waited for; matrix products, arithmetic and copies ran while one was open for 6% of the time, Pallas kernels for 0%

commit v1 on v0

--- a/solution.py
+++ b/solution.py
@@ -112,7 +112,11 @@
         scatter_dimension=0,
         tiled=True,
     )
-    weight_rows = lax.psum(weight_rows, "stream")
+    weight_rows = weight_rows
+    for hop in (1, 2):
+        weight_rows = weight_rows + lax.ppermute(
+            weight_rows, "stream", [(dev, dev ^ hop) for dev in range(4)]
+        )
     return (output[None], carried[None], weight_rows * factor, angle_all * factor, mix_all * factor)
 
 

time: 819 us -> 774 us (0.945)
  waiting for transfers between devices: 489 us -> 440 us
    psum x1 -> x0, waiting for transfers between devices: 43.9 us -> none  [body(): weight_rows = lax.psum(weight_rows, 'stream')]
    psum x1, waiting for transfers between devices: 243 us -> 233 us  [body(): lax.psum((jnp.stack([theta, phi]), jnp.stack(mix_rows)), ('stream', 'seq'))]
  transfers between devices with their start and end apart: 29 -> 30, of which waited for: 26 -> 26; matrix products, arithmetic and copies ran while one was open for 6% -> 6% of each run, Pallas kernels for 0% -> 0%
where the time goes in v1:
time: 774 us; the launch traced here: 767 us
  waiting for transfers between devices  440 us (57%)
  starting transfers between devices  128 us (17%)
  blocking collectives  102 us (13%)
  other arithmetic  58.4 us (8%)
  between operations  17.8 us (2%)
  matrix products  13.3 us (2%)
    psum x1, waiting for transfers between devices, body(): lax.psum((jnp.stack([theta, phi]), jnp.stack(mix_rows)), ('stream', 'seq'))  233 us
    ppermute x26, waiting for transfers between devices, from_behind(): return lax.ppermute(block, axis, route)  201 us
    ppermute x26, starting transfers between devices, from_behind(): return lax.ppermute(block, axis, route)  125 us
    psum x1, blocking collectives, body(): lax.psum((jnp.stack([theta, phi]), jnp.stack(mix_rows)), ('stream', 'seq'))  102 us
    reduce_sum x10, other arithmetic, body(): jnp.sum(grad_full * (cos_d * plain + sin_d * shifted), axis=0)  22.1 us
  transfers between devices with their start and end apart: 30, of which 26 were waited for; matrix products, arithmetic and copies ran while one was open for 6% of the time, Pallas kernels for 0%

profile of v1, /device:TPU:8, one launch (start us, length us, event | category | flops | bytes accessed | tf_op | source)
XLA Modules:
  0.0 767.1 jit_solution(10923832567938985907)
XLA Ops:
  8.9 1.9 collective-permute-start
  11.9 1.9 slice_cosine_fusion.1
  17.4 3.6 collective-permute-start.1
  23.6 1.9 collective-permute-start.2
  25.5 3.1 collective-permute-done.2
  29.6 1.9 collective-permute-start.3
  31.6 3.3 collective-permute-done.3
  35.9 2.1 collective-permute-start.4
  38.0 3.6 collective-permute-done.4
  42.5 1.9 collective-permute-start.5
  44.4 4.3 collective-permute-done.5
  49.7 1.9 collective-permute-start.6
  51.6 5.8 collective-permute-done.6
  58.4 2.1 collective-permute-start.7
  60.5 8.6 %collective-permute-done.7 = bf16[128,2048]{1,0:T(8,128)(2,1)S(1)} collective-permute-done((bf16[128,2048]{1,0:T(8,128)(2,1)S(1)}, bf16[128,2048]{1,0:T(8,128)(2,1)S(1)}, u32[]{:S(2)}, u32[]{:S(2)}) %collective-permute-start.7) | collective-permute-done | bytes 524320 | tf_op jit(solution)/shard_map/ppermute | solution.py:10
  70.1 3.5 collective-permute-start.8
  73.6 11.4 %collective-permute-done.8 = bf16[128,2048]{1,0:T(8,128)(2,1)S(1)} collective-permute-done((bf16[128,2048]{1,0:T(8,128)(2,1)S(1)}, bf16[128,2048]{1,0:T(8,128)(2,1)S(1)}, u32[]{:S(2)}, u32[]{:S(2)}) %collective-permute-start.8) | collective-permute-done | bytes 524320 | tf_op jit(solution)/shard_map/ppermute | solution.py:10
  86.0 15.0 %collective-permute-start.9 = (bf16[128,2048]{1,0:T(8,128)(2,1)S(1)}, bf16[128,2048]{1,0:T(8,128)(2,1)S(1)}, u32[]{:S(2)}, u32[]{:S(2)}) collective-permute-start(bf16[128,2048]{1,0:T(8,128)(2,1)S(1)} %fusion.250), channel_id=1, source_target_pairs={{0,4},{1,5},{2,6},{3,7},{4,8},{5,9},{6,10},{7,11},{8,12},{9,13},{1... | collective-permute-start | bytes 1572872 | tf_op jit(solution)/shard_map/ppermute | solution.py:10
  101.0 7.5 collective-permute-done.9
  109.4 4.4 collective-permute-start.10
  113.7 6.6 collective-permute-done.10
  121.3 14.6 %collective-permute-start.11 = (bf16[128,2048]{1,0:T(8,128)(2,1)S(1)}, bf16[128,2048]{1,0:T(8,128)(2,1)S(1)}, u32[]{:S(2)}, u32[]{:S(2)}) collective-permute-start(bf16[128,2048]{1,0:T(8,128)(2,1)S(1)} %fusion.254), channel_id=1, source_target_pairs={{0,16},{1,17},{2,18},{3,19},{4,20},{5,21},{6,22},{7,23},{8,24},{9,... | collective-permute-start | bytes 1572872 | tf_op jit(solution)/shard_map/ppermute | solution.py:10
  135.9 8.1 %collective-permute-done.11 = bf16[128,2048]{1,0:T(8,128)(2,1)S(1)} collective-permute-done((bf16[128,2048]{1,0:T(8,128)(2,1)S(1)}, bf16[128,2048]{1,0:T(8,128)(2,1)S(1)}, u32[]{:S(2)}, u32[]{:S(2)}) %collective-permute-start.11) | collective-permute-done | bytes 524320 | tf_op jit(solution)/shard_map/ppermute | solution.py:10
  144.9 31.3 %collective-permute-start.12 = (bf16[128,2048]{1,0:T(8,128)(2,1)S(1)}, bf16[128,2048]{1,0:T(8,128)(2,1)S(1)}, u32[]{:S(2)}, u32[]{:S(2)}) collective-permute-start(bf16[128,2048]{1,0:T(8,128)(2,1)S(1)} %fusion.256), channel_id=1, source_target_pairs={{0,32},{1,33},{2,34},{3,35},{4,36},{5,37},{6,38},{7,39},{8,40},{9,... | collective-permute-start | bytes 1572872 | tf_op jit(solution)/shard_map/ppermute | solution.py:10
  176.3 2.9 convolution_convert_fusion
  179.4 7.8 %collective-permute-done.12 = bf16[128,2048]{1,0:T(8,128)(2,1)S(1)} collective-permute-done((bf16[128,2048]{1,0:T(8,128)(2,1)S(1)}, bf16[128,2048]{1,0:T(8,128)(2,1)S(1)}, u32[]{:S(2)}, u32[]{:S(2)}) %collective-permute-start.12) | collective-permute-done | bytes 524320 | tf_op jit(solution)/shard_map/ppermute | solution.py:10
  188.4 7.4 fusion.97
  197.0 8.1 %fusion.288 = f32[2048,2048]{1,0:T(8,128)} fusion(bf16[1,128,2048]{2,1,0:T(8,128)(2,1)S(1)} %copy-done, f32[128,2048]{1,0:T(8,128)S(1)} %get-tuple-element.55), kind=kOutput, calls=%fused_computation.471 | convolution fusion | flops 1076101120 | bytes 18350080 | tf_op jit(solution)/shard_map/dot_general | solution.py:108
  207.9 19.4 %collective-permute-done.13 = bf16[128,2048]{1,0:T(8,128)(2,1)S(1)} collective-permute-done((bf16[128,2048]{1,0:T(8,128)(2,1)S(1)}, bf16[128,2048]{1,0:T(8,128)(2,1)S(1)}, u32[]{:S(2)}, u32[]{:S(2)}) %collective-permute-start.13) | collective-permute-done | bytes 524320 | tf_op jit(solution)/shard_map/ppermute | solution.py:10
  230.6 26.2 %collective-permute-done.14 = bf16[128,2048]{1,0:T(8,128)(2,1)S(1)} collective-permute-done((bf16[128,2048]{1,0:T(8,128)(2,1)S(1)}, bf16[128,2048]{1,0:T(8,128)(2,1)S(1)}, u32[]{:S(2)}, u32[]{:S(2)}) %collective-permute-start.14) | collective-permute-done | bytes 524320 | tf_op jit(solution)/shard_map/ppermute | solution.py:10
  260.5 13.7 %collective-permute-done.15 = bf16[128,2048]{1,0:T(8,128)(2,1)S(1)} collective-permute-done((bf16[128,2048]{1,0:T(8,128)(2,1)S(1)}, bf16[128,2048]{1,0:T(8,128)(2,1)S(1)}, u32[]{:S(2)}, u32[]{:S(2)}) %collective-permute-start.15) | collective-permute-done | bytes 524320 | tf_op jit(solution)/shard_map/ppermute | solution.py:10
  275.3 3.1 fusion.270
  279.7 19.8 %collective-permute-done.16 = bf16[128,2048]{1,0:T(8,128)(2,1)S(1)} collective-permute-done((bf16[128,2048]{1,0:T(8,128)(2,1)S(1)}, bf16[128,2048]{1,0:T(8,128)(2,1)S(1)}, u32[]{:S(2)}, u32[]{:S(2)}) %collective-permute-start.16) | collective-permute-done | bytes 524320 | tf_op jit(solution)/shard_map/ppermute | solution.py:10
  299.9 3.1 fusion.269
  302.9 10.8 %collective-permute-start.17 = (bf16[128,2048]{1,0:T(8,128)(2,1)S(1)}, bf16[128,2048]{1,0:T(8,128)(2,1)S(1)}, u32[]{:S(2)}, u32[]{:S(2)}) collective-permute-start(bf16[128,2048]{1,0:T(8,128)(2,1)S(1)} %get-tuple-element.57), channel_id=1, source_target_pairs={{2,0},{3,1},{4,2},{5,3},{6,4},{7,5},{8,6},{9,7},{10,8},{11,9},{12,... | collective-permute-start | bytes 1572872 | tf_op jit(solution)/shard_map/ppermute | solution.py:10
  313.7 22.7 %collective-permute-done.17 = bf16[128,2048]{1,0:T(8,128)(2,1)S(1)} collective-permute-done((bf16[128,2048]{1,0:T(8,128)(2,1)S(1)}, bf16[128,2048]{1,0:T(8,128)(2,1)S(1)}, u32[]{:S(2)}, u32[]{:S(2)}) %collective-permute-start.17) | collective-permute-done | bytes 524320 | tf_op jit(solution)/shard_map/ppermute | solution.py:10
  336.9 3.0 fusion.268
  339.9 1.9 collective-permute-start.18
  341.8 6.7 collective-permute-done.18
  348.9 2.2 fusion.267
  351.1 4.2 collective-permute-start.19
  355.4 3.9 collective-permute-done.19
  359.6 2.2 fusion.266
  361.8 4.2 collective-permute-start.20
  366.1 4.8 collective-permute-done.20
  371.2 1.5 fusion.265
  372.8 3.9 collective-permute-start.21
  376.8 4.5 collective-permute-done.21
  381.7 1.6 fusion.264
  383.3 1.9 collective-permute-start.22
  385.2 3.6 collective-permute-done.22
  389.1 1.8 fusion.263
  390.9 1.9 collective-permute-start.23
  393.0 3.1 collective-permute-done.23
  396.5 1.8 fusion.262
  398.4 2.1 collective-permute-start.24
  400.5 2.3 fusion
  404.2 1.8 fusion.261
  406.0 2.0 collective-permute-start.25
  408.1 102.1 %psum.14 = f32[2,2048]{1,0:T(2,128)S(1)} all-reduce(f32[2,2048]{1,0:T(2,128)S(1)} %pad_maximum_fusion.7), channel_id=1, replica_groups=mesh['stream'=4,'seq'=64] {'stream','seq'}, use_global_device_ids=true, to_apply=%region_29.30 | all-reduce | flops 4096 | bytes 32768 | tf_op jit(solution)/shard_map/psum | solution.py:106
  514.7 6.2 collective-permute-done.26
  521.9 2.2 collective-permute-start.27
  524.2 233.0 %all-reduce.2.cloned.1.call-done = f32[14,2048]{1,0:T(8,128)} async-done(((f32[14,2048]{1,0:T(8,128)}), f32[14,2048]{1,0:T(8,128)}) %all-reduce.2.cloned.1.call-update) | async-done | bytes 114704 | tf_op jit(solution)/shard_map/psum | solution.py:106
  757.1 1.6 broadcast_multiply_fusion
  (288 shorter events, 41.9 us)
Async XLA Ops:
  8.0 168.2 %copy-start = (bf16[1,128,2048]{2,1,0:T(8,128)(2,1)S(1)}, bf16[1,128,2048]{2,1,0:T(8,128)(2,1)}, u32[]{:S(2)}) copy-start(bf16[1,128,2048]{2,1,0:T(8,128)(2,1)} %param.7) | copy-start | bytes 1572868
  8.0 504.5 %reduce-scatter.2.cloned.1.call-start = ((), (), s32[]{:S(2)}) async-start(), calls=%async_computation.1 | async-start | bytes 17039360 | tf_op jit(solution)/shard_map/reduce_scatter | solution.py:107
  8.9 7.1 collective-permute-start
  17.4 5.1 collective-permute-start.1
  23.6 5.1 collective-permute-start.2
  28.6 159.5 %copy-start.65 = (bf16[4,2048]{1,0:T(4,128)(2,1)}, bf16[4,2048]{1,0:T(4,128)(2,1)S(1)}, u32[]{:S(2)}) copy-start(bf16[4,2048]{1,0:T(4,128)(2,1)S(1)} %collective-permute-done.2) | copy-start | bytes 49156
  29.6 5.2 collective-permute-start.3
  31.6 156.6 %copy-start.22 = (bf16[120,2048]{1,0:T(8,128)(2,1)}, bf16[120,2048]{1,0:T(8,128)(2,1)S(1)}, u32[]{:S(2)}) copy-start(bf16[120,2048]{1,0:T(8,128)(2,1)S(1)} %slice.205) | copy-start | bytes 1474564
  34.8 153.4 %copy-start.55 = (bf16[8,2048]{1,0:T(8,128)(2,1)}, bf16[8,2048]{1,0:T(8,128)(2,1)S(1)}, u32[]{:S(2)}) copy-start(bf16[8,2048]{1,0:T(8,128)(2,1)S(1)} %collective-permute-done.3) | copy-start | bytes 98308
  34.8 141.4 %slice-start = ((s8[8388608]{0:T(1024)(128)(4,1)}), s8[4194304]{0:T(1024)(128)(4,1)S(1)}, s32[]{:S(2)}) async-start(s8[8388608]{0:T(1024)(128)(4,1)} %bitcast.103), calls=%async_computation.3 | async-start | bytes 8388608
  35.9 5.7 collective-permute-start.4
  38.0 150.2 %copy-start.24 = (bf16[112,2048]{1,0:T(8,128)(2,1)}, bf16[112,2048]{1,0:T(8,128)(2,1)S(1)}, u32[]{:S(2)}) copy-start(bf16[112,2048]{1,0:T(8,128)(2,1)S(1)} %slice.207) | copy-start | bytes 1376260
  41.6 146.6 %copy-start.53 = (bf16[16,2048]{1,0:T(8,128)(2,1)}, bf16[16,2048]{1,0:T(8,128)(2,1)S(1)}, u32[]{:S(2)}) copy-start(bf16[16,2048]{1,0:T(8,128)(2,1)S(1)} %collective-permute-done.4) | copy-start | bytes 196612
  42.4 145.8 %copy-start.1 = (bf16[128,2048]{1,0:T(8,128)(2,1)}, bf16[128,2048]{1,0:T(8,128)(2,1)S(1)}, u32[]{:S(2)}) copy-start(bf16[128,2048]{1,0:T(8,128)(2,1)S(1)} %fusion.242) | copy-start | bytes 1572868
  42.5 6.3 collective-permute-start.5
  48.8 139.5 %copy-start.51 = (bf16[32,2048]{1,0:T(8,128)(2,1)}, bf16[32,2048]{1,0:T(8,128)(2,1)S(1)}, u32[]{:S(2)}) copy-start(bf16[32,2048]{1,0:T(8,128)(2,1)S(1)} %collective-permute-done.5) | copy-start | bytes 393220
  49.6 138.6 %copy-start.3 = (bf16[128,2048]{1,0:T(8,128)(2,1)}, bf16[128,2048]{1,0:T(8,128)(2,1)S(1)}, u32[]{:S(2)}) copy-start(bf16[128,2048]{1,0:T(8,128)(2,1)S(1)} %fusion.244) | copy-start | bytes 1572868
  49.7 138.6 %copy-start.43 = (bf16[64,2048]{1,0:T(8,128)(2,1)}, bf16[64,2048]{1,0:T(8,128)(2,1)S(1)}, u32[]{:S(2)}) copy-start(bf16[64,2048]{1,0:T(8,128)(2,1)S(1)} %get-tuple-element.69) | copy-start | bytes 786436
  49.7 7.7 %collective-permute-start.6 = (bf16[64,2048]{1,0:T(8,128)(2,1)S(1)}, bf16[64,2048]{1,0:T(8,128)(2,1)S(1)}, u32[]{:S(2)}, u32[]{:S(2)}) collective-permute-start(bf16[64,2048]{1,0:T(8,128)(2,1)S(1)} %get-tuple-element.68), channel_id=1, source_target_pairs={{0,1},{1,2},{2,3},{3,4},{4,5},{5,6},{6,7},{7,8},{8,9},{9,10},{10,1... | collective-permute-start | bytes 786440 | tf_op jit(solution)/shard_map/ppermute | solution.py:10
  57.4 130.9 %copy-start.47 = (bf16[64,2048]{1,0:T(8,128)(2,1)}, bf16[64,2048]{1,0:T(8,128)(2,1)S(1)}, u32[]{:S(2)}) copy-start(bf16[64,2048]{1,0:T(8,128)(2,1)S(1)} %collective-permute-done.6) | copy-start | bytes 786436
  57.4 118.8 %slice-start.1 = ((s8[8388608]{0:T(1024)(128)(4,1)}), s8[4194304]{0:T(1024)(128)(4,1)S(1)}, s32[]{:S(2)}) async-start(s8[8388608]{0:T(1024)(128)(4,1)} %bitcast.103), calls=%async_computation.4 | async-start | bytes 8388608
  58.4 129.9 %copy-start.18 = (bf16[128,2048]{1,0:T(8,128)(2,1)}, bf16[128,2048]{1,0:T(8,128)(2,1)S(1)}, u32[]{:S(2)}) copy-start(bf16[128,2048]{1,0:T(8,128)(2,1)S(1)} %fusion.246) | copy-start | bytes 1572868
  58.4 10.6 %collective-permute-start.7 = (bf16[128,2048]{1,0:T(8,128)(2,1)S(1)}, bf16[128,2048]{1,0:T(8,128)(2,1)S(1)}, u32[]{:S(2)}, u32[]{:S(2)}) collective-permute-start(bf16[128,2048]{1,0:T(8,128)(2,1)S(1)} %fusion.246), channel_id=1, source_target_pairs={{0,1},{1,2},{2,3},{3,4},{4,5},{5,6},{6,7},{7,8},{8,9},{9,10},{10,1... | collective-permute-start | bytes 1572872 | tf_op jit(solution)/shard_map/ppermute | solution.py:10
  69.1 119.2 %copy-start.39 = (bf16[128,2048]{1,0:T(8,128)(2,1)}, bf16[128,2048]{1,0:T(8,128)(2,1)S(1)}, u32[]{:S(2)}) copy-start(bf16[128,2048]{1,0:T(8,128)(2,1)S(1)} %collective-permute-done.7) | copy-start | bytes 1572868
  69.1 110.1 %copy-start.87 = (f32[14,2048]{1,0:T(8,128)S(1)}, f32[14,2048]{1,0:T(8,128)}, u32[]{:S(2)}) copy-start(f32[14,2048]{1,0:T(8,128)} %param.10) | copy-start | bytes 344068
  70.0 118.2 %copy-start.7 = (bf16[128,2048]{1,0:T(8,128)(2,1)}, bf16[128,2048]{1,0:T(8,128)(2,1)S(1)}, u32[]{:S(2)}) copy-start(bf16[128,2048]{1,0:T(8,128)(2,1)S(1)} %fusion.248) | copy-start | bytes 1572868
  70.1 14.9 %collective-permute-start.8 = (bf16[128,2048]{1,0:T(8,128)(2,1)S(1)}, bf16[128,2048]{1,0:T(8,128)(2,1)S(1)}, u32[]{:S(2)}, u32[]{:S(2)}) collective-permute-start(bf16[128,2048]{1,0:T(8,128)(2,1)S(1)} %fusion.248), channel_id=1, source_target_pairs={{0,2},{1,3},{2,4},{3,5},{4,6},{5,7},{6,8},{7,9},{8,10},{9,11},{10,... | collective-permute-start | bytes 1572872 | tf_op jit(solution)/shard_map/ppermute | solution.py:10
  85.0 103.3 %copy-start.29 = (bf16[128,2048]{1,0:T(8,128)(2,1)}, bf16[128,2048]{1,0:T(8,128)(2,1)S(1)}, u32[]{:S(2)}) copy-start(bf16[128,2048]{1,0:T(8,128)(2,1)S(1)} %collective-permute-done.8) | copy-start | bytes 1572868
  85.9 109.9 %copy-start.11 = (bf16[128,2048]{1,0:T(8,128)(2,1)}, bf16[128,2048]{1,0:T(8,128)(2,1)S(1)}, u32[]{:S(2)}) copy-start(bf16[128,2048]{1,0:T(8,128)(2,1)S(1)} %fusion.250) | copy-start | bytes 1572868
  85.9 102.4 %copy-start.5 = (bf16[1,128,2048]{2,1,0:T(8,128)(2,1)S(1)}, bf16[1,128,2048]{2,1,0:T(8,128)(2,1)}, u32[]{:S(2)}) copy-start(bf16[1,128,2048]{2,1,0:T(8,128)(2,1)} %param.6) | copy-start | bytes 1572868
  85.9 102.4 %copy-start.16 = (bf16[127,2048]{1,0:T(8,128)(2,1)S(1)}, bf16[127,2048]{1,0:T(8,128)(2,1)}, u32[]{:S(2)}) copy-start(bf16[127,2048]{1,0:T(8,128)(2,1)} %copy-done.15) | copy-start | bytes 1560580
  85.9 102.4 %copy-start.26 = (f32[1,2048]{1,0:T(1,128)S(1)}, f32[1,2048]{1,0:T(1,128)}, u32[]{:S(2)}) copy-start(f32[1,2048]{1,0:T(1,128)} %get-tuple-element.84) | copy-start | bytes 24580
  85.9 102.4 %copy-start.49 = (f32[1,2048]{1,0:T(1,128)S(1)}, f32[1,2048]{1,0:T(1,128)}, u32[]{:S(2)}) copy-start(f32[1,2048]{1,0:T(1,128)} %get-tuple-element.85) | copy-start | bytes 24580
  85.9 102.4 %copy-start.89 = (bf16[1,2048]{1,0:T(2,128)(2,1)S(1)}, bf16[1,2048]{1,0:T(2,128)(2,1)}, u32[]{:S(2)}) copy-start(bf16[1,2048]{1,0:T(2,128)(2,1)} %copy-done.88) | copy-start | bytes 12292
  86.0 22.5 %collective-permute-start.9 = (bf16[128,2048]{1,0:T(8,128)(2,1)S(1)}, bf16[128,2048]{1,0:T(8,128)(2,1)S(1)}, u32[]{:S(2)}, u32[]{:S(2)}) collective-permute-start(bf16[128,2048]{1,0:T(8,128)(2,1)S(1)} %fusion.250), channel_id=1, source_target_pairs={{0,4},{1,5},{2,6},{3,7},{4,8},{5,9},{6,10},{7,11},{8,12},{9,13},{1... | collective-permute-start | bytes 1572872 | tf_op jit(solution)/shard_map/ppermute | solution.py:10
  109.4 11.0 %collective-permute-start.10 = (bf16[128,2048]{1,0:T(8,128)(2,1)S(1)}, bf16[128,2048]{1,0:T(8,128)(2,1)S(1)}, u32[]{:S(2)}, u32[]{:S(2)}) collective-permute-start(bf16[128,2048]{1,0:T(8,128)(2,1)S(1)} %fusion.252), channel_id=1, source_target_pairs={{0,8},{1,9},{2,10},{3,11},{4,12},{5,13},{6,14},{7,15},{8,16},{9,17... | collective-permute-start | bytes 1572872 | tf_op jit(solution)/shard_map/ppermute | solution.py:10
  121.3 22.6 %collective-permute-start.11 = (bf16[128,2048]{1,0:T(8,128)(2,1)S(1)}, bf16[128,2048]{1,0:T(8,128)(2,1)S(1)}, u32[]{:S(2)}, u32[]{:S(2)}) collective-permute-start(bf16[128,2048]{1,0:T(8,128)(2,1)S(1)} %fusion.254), channel_id=1, source_target_pairs={{0,16},{1,17},{2,18},{3,19},{4,20},{5,21},{6,22},{7,23},{8,24},{9,... | collective-permute-start | bytes 1572872 | tf_op jit(solution)/shard_map/ppermute | solution.py:10
  144.9 42.4 %collective-permute-start.12 = (bf16[128,2048]{1,0:T(8,128)(2,1)S(1)}, bf16[128,2048]{1,0:T(8,128)(2,1)S(1)}, u32[]{:S(2)}, u32[]{:S(2)}) collective-permute-start(bf16[128,2048]{1,0:T(8,128)(2,1)S(1)} %fusion.256), channel_id=1, source_target_pairs={{0,32},{1,33},{2,34},{3,35},{4,36},{5,37},{6,38},{7,39},{8,40},{9,... | collective-permute-start | bytes 1572872 | tf_op jit(solution)/shard_map/ppermute | solution.py:10
  205.2 552.0 %all-reduce.2.cloned.1.call-start = ((), (), s32[]{:S(2)}) async-start(), calls=%async_computation.2 | async-start | bytes 262144 | tf_op jit(solution)/shard_map/psum | solution.py:106
  205.3 94.5 %copy-start.8 = (bf16[128,2048]{1,0:T(8,128)(2,1)S(1)}, bf16[128,2048]{1,0:T(8,128)(2,1)}, u32[]{:S(2)}) copy-start(bf16[128,2048]{1,0:T(8,128)(2,1)} %copy-done.7) | copy-start | bytes 1572868
  206.5 20.8 %collective-permute-start.13 = (bf16[128,2048]{1,0:T(8,128)(2,1)S(1)}, bf16[128,2048]{1,0:T(8,128)(2,1)S(1)}, u32[]{:S(2)}, u32[]{:S(2)}) collective-permute-start(bf16[128,2048]{1,0:T(8,128)(2,1)S(1)} %fusion.189), channel_id=1, source_target_pairs={{32,0},{33,1},{34,2},{35,3},{36,4},{37,5},{38,6},{39,7},{40,8},{41... | collective-permute-start | bytes 1572872 | tf_op jit(solution)/shard_map/ppermute | solution.py:10
  229.3 27.5 %collective-permute-start.14 = (bf16[128,2048]{1,0:T(8,128)(2,1)S(1)}, bf16[128,2048]{1,0:T(8,128)(2,1)S(1)}, u32[]{:S(2)}, u32[]{:S(2)}) collective-permute-start(bf16[128,2048]{1,0:T(8,128)(2,1)S(1)} %fusion.182), channel_id=1, source_target_pairs={{16,0},{17,1},{18,2},{19,3},{20,4},{21,5},{22,6},{23,7},{24,8},{25... | collective-permute-start | bytes 1572872 | tf_op jit(solution)/shard_map/ppermute | solution.py:10
  259.0 15.1 %collective-permute-start.15 = (bf16[128,2048]{1,0:T(8,128)(2,1)S(1)}, bf16[128,2048]{1,0:T(8,128)(2,1)S(1)}, u32[]{:S(2)}, u32[]{:S(2)}) collective-permute-start(bf16[128,2048]{1,0:T(8,128)(2,1)S(1)} %fusion.175), channel_id=1, source_target_pairs={{8,0},{9,1},{10,2},{11,3},{12,4},{13,5},{14,6},{15,7},{16,8},{17,9... | collective-permute-start | bytes 1572872 | tf_op jit(solution)/shard_map/ppermute | solution.py:10
  278.4 21.1 %collective-permute-start.16 = (bf16[128,2048]{1,0:T(8,128)(2,1)S(1)}, bf16[128,2048]{1,0:T(8,128)(2,1)S(1)}, u32[]{:S(2)}, u32[]{:S(2)}) collective-permute-start(bf16[128,2048]{1,0:T(8,128)(2,1)S(1)} %get-tuple-element.56), channel_id=1, source_target_pairs={{4,0},{5,1},{6,2},{7,3},{8,4},{9,5},{10,6},{11,7},{12,8},{13,9},{1... | collective-permute-start | bytes 1572872 | tf_op jit(solution)/shard_map/ppermute | solution.py:10
  302.9 33.5 %collective-permute-start.17 = (bf16[128,2048]{1,0:T(8,128)(2,1)S(1)}, bf16[128,2048]{1,0:T(8,128)(2,1)S(1)}, u32[]{:S(2)}, u32[]{:S(2)}) collective-permute-start(bf16[128,2048]{1,0:T(8,128)(2,1)S(1)} %get-tuple-element.57), channel_id=1, source_target_pairs={{2,0},{3,1},{4,2},{5,3},{6,4},{7,5},{8,6},{9,7},{10,8},{11,9},{12,... | collective-permute-start | bytes 1572872 | tf_op jit(solution)/shard_map/ppermute | solution.py:10
  339.9 8.6 %collective-permute-start.18 = (bf16[128,2048]{1,0:T(8,128)(2,1)S(1)}, bf16[128,2048]{1,0:T(8,128)(2,1)S(1)}, u32[]{:S(2)}, u32[]{:S(2)}) collective-permute-start(bf16[128,2048]{1,0:T(8,128)(2,1)S(1)} %get-tuple-element.58), channel_id=1, source_target_pairs={{1,0},{2,1},{3,2},{4,3},{5,4},{6,5},{7,6},{8,7},{9,8},{10,9},{11,1... | collective-permute-start | bytes 1572872 | tf_op jit(solution)/shard_map/ppermute | solution.py:10
  351.1 8.1 %collective-permute-start.19 = (bf16[64,2048]{1,0:T(8,128)(2,1)S(1)}, bf16[64,2048]{1,0:T(8,128)(2,1)S(1)}, u32[]{:S(2)}, u32[]{:S(2)}) collective-permute-start(bf16[64,2048]{1,0:T(8,128)(2,1)S(1)} %get-tuple-element.67), channel_id=1, source_target_pairs={{1,0},{2,1},{3,2},{4,3},{5,4},{6,5},{7,6},{8,7},{9,8},{10,9},{11,1... | collective-permute-start | bytes 786440 | tf_op jit(solution)/shard_map/ppermute | solution.py:10
  361.8 9.1 %collective-permute-start.20 = (bf16[32,2048]{1,0:T(8,128)(2,1)S(1)}, bf16[32,2048]{1,0:T(8,128)(2,1)S(1)}, u32[]{:S(2)}, u32[]{:S(2)}) collective-permute-start(bf16[32,2048]{1,0:T(8,128)(2,1)S(1)} %slice.215), channel_id=1, source_target_pairs={{1,0},{2,1},{3,2},{4,3},{5,4},{6,5},{7,6},{8,7},{9,8},{10,9},{11,1... | collective-permute-start | bytes 393224 | tf_op jit(solution)/shard_map/ppermute | solution.py:10
  372.8 8.5 %collective-permute-start.21 = (bf16[16,2048]{1,0:T(8,128)(2,1)S(1)}, bf16[16,2048]{1,0:T(8,128)(2,1)S(1)}, u32[]{:S(2)}, u32[]{:S(2)}) collective-permute-start(bf16[16,2048]{1,0:T(8,128)(2,1)S(1)} %slice.217), channel_id=1, source_target_pairs={{1,0},{2,1},{3,2},{4,3},{5,4},{6,5},{7,6},{8,7},{9,8},{10,9},{11,1... | collective-permute-start | bytes 196616 | tf_op jit(solution)/shard_map/ppermute | solution.py:10
  383.3 5.5 collective-permute-start.22
  390.9 5.2 collective-permute-start.23
  398.3 112.7 %copy-start.91 = (f32[2048]{0:T(1024)S(1)}, f32[2048]{0:T(1024)}, u32[]{:S(2)}) copy-start(f32[2048]{0:T(1024)} %get-tuple-element.17) | copy-start | bytes 24580
  398.3 112.7 %copy-start.92 = (f32[2048]{0:T(1024)S(1)}, f32[2048]{0:T(1024)}, u32[]{:S(2)}) copy-start(f32[2048]{0:T(1024)} %get-tuple-element.52) | copy-start | bytes 24580
  398.3 112.7 %copy-start.93 = (f32[2048]{0:T(1024)S(1)}, f32[2048]{0:T(1024)}, u32[]{:S(2)}) copy-start(f32[2048]{0:T(1024)} %get-tuple-element.19) | copy-start | bytes 24580
  398.3 112.7 %copy-start.94 = (f32[2048]{0:T(1024)S(1)}, f32[2048]{0:T(1024)}, u32[]{:S(2)}) copy-start(f32[2048]{0:T(1024)} %get-tuple-element.49) | copy-start | bytes 24580
  398.4 112.7 %copy-start.95 = (f32[2048]{0:T(1024)S(1)}, f32[2048]{0:T(1024)}, u32[]{:S(2)}) copy-start(f32[2048]{0:T(1024)} %get-tuple-element.21) | copy-start | bytes 24580
  398.4 112.7 %copy-start.96 = (f32[2048]{0:T(1024)S(1)}, f32[2048]{0:T(1024)}, u32[]{:S(2)}) copy-start(f32[2048]{0:T(1024)} %get-tuple-element.46) | copy-start | bytes 24580
  398.4 112.7 %copy-start.97 = (f32[2048]{0:T(1024)S(1)}, f32[2048]{0:T(1024)}, u32[]{:S(2)}) copy-start(f32[2048]{0:T(1024)} %get-tuple-element.23) | copy-start | bytes 24580
  398.4 112.7 %copy-start.98 = (f32[2048]{0:T(1024)S(1)}, f32[2048]{0:T(1024)}, u32[]{:S(2)}) copy-start(f32[2048]{0:T(1024)} %get-tuple-element.25) | copy-start | bytes 24580
  398.4 115.2 %copy-start.28 = (f32[1,2048]{1,0:T(1,128)S(1)}, f32[1,2048]{1,0:T(1,128)}, u32[]{:S(2)}) copy-start(f32[1,2048]{1,0:T(1,128)} %get-tuple-element.84) | copy-start | bytes 24580
  398.4 5.4 collective-permute-start.24
  406.0 107.5 %collective-permute-start.25 = (bf16[1,2048]{1,0:T(2,128)(2,1)S(1)}, bf16[1,2048]{1,0:T(2,128)(2,1)S(1)}, u32[]{:S(2)}, u32[]{:S(2)}) collective-permute-start(bf16[1,2048]{1,0:T(2,128)(2,1)S(1)} %slice.225), channel_id=1, source_target_pairs={{1,0},{2,1},{3,2},{4,3},{5,4},{6,5},{7,6},{8,7},{9,8},{10,9},{11,1... | collective-permute-start | bytes 12296 | tf_op jit(solution)/shard_map/ppermute | solution.py:10
  512.6 8.4 %collective-permute-start.26 = (f32[32,2048]{1,0:T(8,128)}, f32[32,2048]{1,0:T(8,128)S(1)}, u32[]{:S(2)}, u32[]{:S(2)}) collective-permute-start(f32[32,2048]{1,0:T(8,128)} %reduce-scatter.2.cloned.1.call-done), channel_id=1, source_target_pairs={{0,64},{64,0},{128,192},{192,128},{1,65},{65,1},{129,193},{193,129... | collective-permute-start | bytes 786440 | tf_op jit(solution)/shard_map/ppermute | solution.py:117
  521.9 236.8 %collective-permute-start.27 = (f32[32,2048]{1,0:T(8,128)S(1)}, f32[32,2048]{1,0:T(8,128)S(1)}, u32[]{:S(2)}, u32[]{:S(2)}) collective-permute-start(f32[32,2048]{1,0:T(8,128)S(1)} %add.742), channel_id=1, source_target_pairs={{0,128},{64,192},{128,0},{192,64},{1,129},{65,193},{129,1},{193,65... | collective-permute-start | bytes 786440 | tf_op jit(solution)/shard_map/ppermute | solution.py:117
  (69 other events, 3173.3 us)
Sparse Core Ops, SparseCore 0:
  205.3 223.6 reduce-scatter.1
Sparse Core Ops, SparseCore 1:
  512.6 244.4 all-reduce.1
